TPU v7x, 32 devices: a whole 2x2x4 slice. The times are simulated.
32 devices in a mesh: dp: 8 (over z, x), seq: 4 (over y, core).
Axes of the slice: x: 2, y: 2, z: 4, core: 2. Of those that a mesh axis runs over, the one named last changes fastest.
Arguments:
- tokens: bfloat16 [32, 6144], P('dp', 'seq'), may hold values from -6 to 6
- expert_ids: int32 [32, 2], P('dp'), may hold values from 0 to 7, all different within a row; in each aligned block of 4 rows (0 to 3, 4 to 7, ...) at most 2 rows name the same one
- router: bfloat16 [6144, 8], P('seq'), may hold values from -0.21875 to 0.21875
- w_gate: bfloat16 [5, 6144, 16384], P(None, 'seq', 'dp'), may hold values from -0.078125 to 0.078125
- w_up: bfloat16 [5, 6144, 16384], P(None, 'seq', 'dp'), may hold values from -0.078125 to 0.078125
- w_down: bfloat16 [5, 16384, 6144], P(None, 'dp', 'seq'), may hold values from -0.046875 to 0.046875
Outputs:
- mixed: bfloat16 [32, 6144], P('dp', 'seq')
Inputs may be any that keep to these rules, and one draw needn't show every extreme that they name: `expert_ids`: each row names 2 different experts. The 4 tokens of one index of dp name any expert at most 2 times, a bound that some block reaches.
All inputs are finite; a program needn't handle non-finite values.
Results may differ from a plain program's by a relative error of at most 0.0049.
Values may be sent and summed in bfloat16 or wider, within the bound.
No kernel may reach another device: no remote copies, remote signals or barrier semaphores. Data moves between devices by JAX's collectives and lax.ppermute only.
A program may use at most 192 MiB of HBM per device.

v0:
```python
import jax
import jax.numpy as jnp
from jax import lax
from jax.sharding import PartitionSpec as P

MOST = 2


def expert_rows(routes, expert, capacity):
    member = jnp.any(routes == expert, axis=1)
    position = jnp.cumsum(member.astype(jnp.int32)) - 1
    target = jnp.where(member, position, capacity)
    count_all = routes.shape[0]
    row_token = (
        jnp.zeros((capacity,), jnp.int32)
        .at[target]
        .set(jnp.arange(count_all, dtype=jnp.int32), mode="drop")
    )
    live_count = jnp.sum(member.astype(jnp.int32))
    return (row_token, jnp.maximum(position, 0), live_count)


def body(tokens, expert_ids, router, w_gate, w_up, w_down):
    gathered = lax.all_gather(tokens, "dp", axis=0, tiled=True)
    routes = lax.all_gather(expert_ids, "dp", axis=0, tiled=True)
    capacity = MOST * lax.axis_size("dp")
    block_rows = min(128, capacity)
    window_size = w_gate.shape[0]
    buffers = []
    positions = []
    live_blocks = []
    for expert in range(window_size):
        row_token, position, live_count = expert_rows(routes, expert, capacity)
        buffers.append(gathered[row_token])
        positions.append(position)
        live_blocks.append((live_count + block_rows - 1) // block_rows)
    gate_list = []
    up_list = []
    for expert in range(window_size):
        gate_part = jnp.dot(buffers[expert], w_gate[expert], preferred_element_type=jnp.float32)
        up_part = jnp.dot(buffers[expert], w_up[expert], preferred_element_type=jnp.float32)
        gate_list.append(gate_part)
        up_list.append(up_part)
    gate_parts = jnp.stack(gate_list)
    up_parts = jnp.stack(up_list)
    logit_part = jnp.dot(gathered, router, preferred_element_type=jnp.float32)
    gate_sum, up_sum, logits = lax.psum((gate_parts, up_parts, logit_part), "seq")
    hidden = (jax.nn.silu(gate_sum) * up_sum).astype(jnp.bfloat16)
    chosen = jnp.take_along_axis(logits, routes, axis=1)
    share_first = 1.0 / (1.0 + jnp.exp(chosen[:, 1] - chosen[:, 0]))
    share_second = 1.0 / (1.0 + jnp.exp(chosen[:, 0] - chosen[:, 1]))
    partial_value = jnp.zeros((gathered.shape[0], w_down.shape[2]), jnp.float32)
    for expert in range(window_size):
        expert_out = jnp.dot(hidden[expert], w_down[expert], preferred_element_type=jnp.float32)
        weighting = jnp.where(routes[:, 0] == expert, share_first, jnp.float32(0.0))
        weighting = weighting + jnp.where(routes[:, 1] == expert, share_second, jnp.float32(0.0))
        partial_value = partial_value + weighting[:, None] * expert_out[positions[expert]]
    return lax.psum_scatter(partial_value, "dp", scatter_dimension=0, tiled=True).astype(
        jnp.bfloat16
    )


def solution(mesh):
    placed = (
        P("dp", "seq"),
        P("dp", None),
        P("seq", None),
        P(None, "seq", "dp"),
        P(None, "seq", "dp"),
        P(None, "dp", "seq"),
    )
    return jax.shard_map(
        body, mesh=mesh, in_specs=placed, out_specs=P("dp", "seq"), check_vma=False
    )
```

profile of v0, /device:TPU:0, one launch (start us, length us, event | category | flops | bytes accessed | tf_op | source)
XLA Modules:
  0.0 207.5 jit_solution(11027577087069102119)
XLA Ops:
  6.5 22.7 %all-gather = s32[8,4,2]{1,2,0:T(2,128)S(1)} all-gather(s32[1,4,2]{1,2,0:T(2,128)} %bitcast.182), channel_id=1, replica_groups=mesh['dp'=8,'seq'=4] {'dp'}, dimensions={0}, use_global_device_ids=true | all-gather | bytes 288 | tf_op jit(solution)/shard_map/all_gather | solution.py:25
  29.3 0.1 copy.46
  29.4 0.1 copy.61
  29.5 0.1 copy.59
  29.6 0.1 copy.57
  29.7 0.1 copy.63
  29.8 0.1 compare_reduce_fusion
  30.0 0.1 copy.55
  30.1 0.1 copy.54
  30.2 0.1 maximum_reduce_fusion.4
  30.3 0.7 scatter_custom_fusion
  31.0 0.1 copy.60
  31.2 0.1 maximum_reduce_fusion.1
  31.3 0.7 scatter_custom_fusion.3
  32.0 0.1 copy.58
  32.1 0.1 maximum_reduce_fusion.2
  32.3 0.7 scatter_custom_fusion.2
  33.0 0.1 copy.56
  33.1 0.1 maximum_reduce_fusion.3
  33.2 0.7 scatter_custom_fusion.1
  33.9 0.1 copy.62
  34.1 0.1 maximum_reduce_fusion
  34.2 0.7 scatter_custom_fusion.4
  34.9 30.8 %all-gather.1 = bf16[8,4,1536]{2,1,0:T(4,128)(2,1)S(1)} all-gather(bf16[1,4,1536]{2,1,0:T(4,128)(2,1)} %bitcast.176), channel_id=1, replica_groups=mesh['dp'=8,'seq'=4] {'dp'}, dimensions={0}, use_global_device_ids=true | all-gather | bytes 110592 | tf_op jit(solution)/shard_map/all_gather | solution.py:24
  65.7 0.6 gather_fusion.4
  66.3 0.6 gather_fusion.3
  66.9 0.6 gather_fusion.2
  67.5 0.6 gather_fusion.1
  68.1 0.6 gather_fusion
  68.7 3.9 %fusion.48 = f32[5,16,2048]{2,1,0:T(8,128)S(1)} fusion(bf16[16,1536]{1,0:T(8,128)(2,1)S(1)} %gather_fusion, bf16[5,1536,2048]{2,1,0:T(8,128)(2,1)} %param.9), kind=kOutput, calls=%fused_computation.62 | convolution fusion | flops 100663296 | bytes 6471680 | tf_op jit(solution)/shard_map/dot_general | solution.py:40
  72.6 4.4 %fusion.78 = f32[5,16,2048]{2,1,0:T(8,128)S(1)} fusion(bf16[16,1536]{1,0:T(8,128)(2,1)S(1)} %gather_fusion, bf16[5,1536,2048]{2,1,0:T(8,128)(2,1)} %param.10), kind=kOutput, calls=%fused_computation.72 | convolution fusion | flops 100663296 | bytes 6471680 | tf_op jit(solution)/shard_map/dot_general | solution.py:41
  77.0 4.5 %fusion.54 = f32[5,16,2048]{2,1,0:T(8,128)S(1)} fusion(f32[5,16,2048]{2,1,0:T(8,128)S(1)} %fusion.48, bf16[16,1536]{1,0:T(8,128)(2,1)S(1)} %gather_fusion.1, bf16[5,1536,2048]{2,1,0:T(8,128)(2,1)} %param.9), kind=kOutput, calls=%fused_computation.64 | convolution fusion | flops 100663296 | bytes 6471680 | tf_op jit(solution)/shard_map/dot_general | solution.py:40
  81.4 4.5 %fusion.84 = f32[5,16,2048]{2,1,0:T(8,128)S(1)} fusion(f32[5,16,2048]{2,1,0:T(8,128)S(1)} %fusion.78, bf16[16,1536]{1,0:T(8,128)(2,1)S(1)} %gather_fusion.1, bf16[5,1536,2048]{2,1,0:T(8,128)(2,1)} %param.10), kind=kOutput, calls=%fused_computation.74 | convolution fusion | flops 100663296 | bytes 6471680 | tf_op jit(solution)/shard_map/dot_general | solution.py:41
  85.9 3.7 %fusion.60 = f32[5,16,2048]{2,1,0:T(8,128)S(1)} fusion(f32[5,16,2048]{2,1,0:T(8,128)S(1)} %fusion.54, bf16[16,1536]{1,0:T(8,128)(2,1)S(1)} %gather_fusion.2, bf16[5,1536,2048]{2,1,0:T(8,128)(2,1)} %param.9), kind=kOutput, calls=%fused_computation.66 | convolution fusion | flops 100663296 | bytes 6471680 | tf_op jit(solution)/shard_map/dot_general | solution.py:40
  89.6 0.9 fusion.90
  90.6 3.7 %fusion.66 = f32[5,16,2048]{2,1,0:T(8,128)S(1)} fusion(f32[5,16,2048]{2,1,0:T(8,128)S(1)} %fusion.60, bf16[16,1536]{1,0:T(8,128)(2,1)S(1)} %gather_fusion.3, bf16[5,1536,2048]{2,1,0:T(8,128)(2,1)} %param.9), kind=kOutput, calls=%fused_computation.68 | convolution fusion | flops 100663296 | bytes 6471680 | tf_op jit(solution)/shard_map/dot_general | solution.py:40
  94.3 0.9 fusion.96
  95.2 3.7 %fusion.72 = f32[5,16,2048]{2,1,0:T(8,128)S(1)} fusion(f32[5,16,2048]{2,1,0:T(8,128)S(1)} %fusion.66, bf16[16,1536]{1,0:T(8,128)(2,1)S(1)} %gather_fusion.4, bf16[5,1536,2048]{2,1,0:T(8,128)(2,1)} %param.9), kind=kOutput, calls=%fused_computation.70 | convolution fusion | flops 100663296 | bytes 6471680 | tf_op jit(solution)/shard_map/dot_general | solution.py:40
  99.0 0.9 fusion.102
  99.9 0.9 copy-done.2
  100.9 0.1 copy.51
  101.0 0.1 reshape.260
  101.1 0.1 fusion.120
  101.2 5.7 %psum.21 = f32[32,8]{0,1:T(8,128)S(1)} all-reduce(f32[32,8]{0,1:T(8,128)S(1)} %fusion.120), channel_id=1, replica_groups=mesh['dp'=8,'seq'=4] {'seq'}, use_global_device_ids=true, to_apply=%region_0.0 | all-reduce | flops 256 | bytes 2048 | tf_op jit(solution)/shard_map/psum | solution.py:47
  106.9 0.7 gather_fusion.10
  107.6 0.1 reshape.263
  107.8 0.6 dynamic-slice
  109.1 0.1 add_divide_fusion.1
  109.2 0.3 add_reduce_fusion.4
  109.4 28.0 %all-reduce.5.cloned.1.call-done = (f32[5,16,2048]{2,1,0:T(8,128)}, f32[5,16,2048]{2,1,0:T(8,128)}) async-done(((f32[5,16,2048]{2,1,0:T(8,128)}, f32[5,16,2048]{2,1,0:T(8,128)}), (f32[5,16,2048]{2,1,0:T(8,128)}, f32[5,16,2048]{2,1,0:T(8,128)})) %all-reduce.5.cloned.1.call-update) | async-done | bytes 1310736 | tf_op jit(solution)/shard_map/psum | solution.py:47
  137.4 1.5 multiply_convert_fusion
  138.9 3.7 %fusion = f32[16,1536]{1,0:T(8,128)S(1)} fusion(bf16[5,2048,1536]{2,1,0:T(8,128)(2,1)} %param.11, bf16[5,16,2048]{2,1,0:T(8,128)(2,1)S(1)} %multiply_convert_fusion), kind=kOutput, calls=%fused_computation.16 | convolution fusion | flops 100663296 | bytes 6455296 | tf_op jit(solution)/shard_map/dot_general | solution.py:54
  142.6 3.7 %fusion.2 = f32[16,1536]{1,0:T(8,128)S(1)} fusion(bf16[5,2048,1536]{2,1,0:T(8,128)(2,1)} %param.11, bf16[5,16,2048]{2,1,0:T(8,128)(2,1)S(1)} %multiply_convert_fusion), kind=kOutput, calls=%fused_computation.18 | convolution fusion | flops 100663296 | bytes 6455296 | tf_op jit(solution)/shard_map/dot_general | solution.py:54
  146.3 3.7 %fusion.4 = f32[16,1536]{1,0:T(8,128)S(1)} fusion(bf16[5,2048,1536]{2,1,0:T(8,128)(2,1)} %param.11, bf16[5,16,2048]{2,1,0:T(8,128)(2,1)S(1)} %multiply_convert_fusion), kind=kOutput, calls=%fused_computation.20 | convolution fusion | flops 100663296 | bytes 6455296 | tf_op jit(solution)/shard_map/dot_general | solution.py:54
  150.0 3.7 %fusion.6 = f32[16,1536]{1,0:T(8,128)S(1)} fusion(bf16[5,2048,1536]{2,1,0:T(8,128)(2,1)} %param.11, bf16[5,16,2048]{2,1,0:T(8,128)(2,1)S(1)} %multiply_convert_fusion), kind=kOutput, calls=%fused_computation.22 | convolution fusion | flops 100663296 | bytes 6455296 | tf_op jit(solution)/shard_map/dot_general | solution.py:54
  153.7 3.7 %fusion.8 = f32[16,1536]{1,0:T(8,128)S(1)} fusion(bf16[5,2048,1536]{2,1,0:T(8,128)(2,1)} %param.11, bf16[5,16,2048]{2,1,0:T(8,128)(2,1)S(1)} %multiply_convert_fusion), kind=kOutput, calls=%fused_computation.24 | convolution fusion | flops 100663296 | bytes 6455296 | tf_op jit(solution)/shard_map/dot_general | solution.py:54
  157.4 0.6 gather_fusion.9
  158.1 0.6 gather_fusion.8
  158.7 0.6 gather_fusion.7
  159.3 0.6 gather_fusion.5
  160.0 0.6 gather_fusion.6
  160.6 0.1 multiply_add_fusion
  160.8 39.3 %all-reduce.6 = bf16[32,1536]{1,0:T(8,128)(2,1)S(1)} all-reduce(f32[32,1536]{1,0:T(8,128)S(1)} %multiply_add_fusion), channel_id=2, replica_groups=mesh['dp'=8,'seq'=4] {'dp'}, use_global_device_ids=true, to_apply=%region_18.19.clone | all-reduce | flops 49152 | bytes 294912
  200.0 0.6 dynamic-slice_convert_fusion
  (45 shorter events, 0.6 us)
Async XLA Ops:
  6.5 94.6 %copy-start = (bf16[1536,8]{0,1:T(8,128)(2,1)S(1)}, bf16[1536,8]{0,1:T(8,128)(2,1)}, u32[]{:S(2)}) copy-start(bf16[1536,8]{0,1:T(8,128)(2,1)} %param.8) | copy-start | bytes 73732
  6.5 130.9 %all-reduce.5.cloned.1.call-start = ((), (), s32[]{:S(2)}) async-start(), calls=%async_computation | async-start | bytes 2621440 | tf_op jit(solution)/shard_map/psum | solution.py:47
  68.7 20.9 %copy-start.1 = (bf16[5,1536,2048]{2,1,0:T(8,128)(2,1)S(1)}, bf16[5,1536,2048]{2,1,0:T(8,128)(2,1)}, u32[]{:S(2)}) copy-start(bf16[5,1536,2048]{2,1,0:T(8,128)(2,1)} %param.10) | copy-start | bytes 94371840
  81.4 26.3 %copy-start.4 = (u32[32]{0:T(128)S(1)}, u32[32]{0:T(128)}, u32[]{:S(2)}) copy-start(u32[32]{0:T(128)} %constant.79) | copy-start | bytes 388
  99.0 0.9 copy-start.3
  99.9 0.9 copy-start.2
Sparse Core Ops, SparseCore 0:
  100.9 36.4 all-reduce.4
where the time goes:
time: 208 us; the launch traced here: 207 us
  blocking collectives  98.3 us (47%)
  matrix products  49.9 us (24%)
  waiting for transfers between devices  28 us (13%)
  between operations  14.4 us (7%)
  local copies, waits for them, and re-layouts  13.9 us (7%)
  other arithmetic  3.05 us (1%)
    unnamed x1, blocking collectives  39.3 us
    all_gather x1, blocking collectives, body(): gathered = lax.all_gather(tokens, 'dp', axis=0, tiled=True)  30.8 us
    psum x1, waiting for transfers between devices, body(): lax.psum((gate_parts, up_parts, logit_part), 'seq')  28 us
    all_gather x1, blocking collectives, body(): routes = lax.all_gather(expert_ids, 'dp', axis=0, tiled=True)  22.7 us
    dot_general x5, matrix products, body(): jnp.dot(buffers[expert], w_gate[expert], preferred_element_type=jnp.float32)  19.5 us
    dot_general x5, matrix products, body(): jnp.dot(hidden[expert], w_down[expert], preferred_element_type=jnp.float32)  18.6 us
    dot_general x5, matrix products, body(): jnp.dot(buffers[expert], w_up[expert], preferred_element_type=jnp.float32)  11.6 us
    psum x1, blocking collectives, body(): lax.psum((gate_parts, up_parts, logit_part), 'seq')  5.66 us
  transfers between devices with their start and end apart: 1, of which 1 were waited for; matrix products, arithmetic and copies ran while one was open for 1% of the time, Pallas kernels for 0%

commit v1 on v0

--- a/solution.py
+++ b/solution.py
@@ -22,7 +22,14 @@
 
 def body(tokens, expert_ids, router, w_gate, w_up, w_down):
     gathered = lax.all_gather(tokens, "dp", axis=0, tiled=True)
-    routes = lax.all_gather(expert_ids, "dp", axis=0, tiled=True)
+    devices = lax.axis_size("dp")
+    forward = [(i, (i + 1) % devices) for i in range(devices)]
+    parts = [expert_ids]
+    for stride in range(1, devices):
+        parts = [lax.ppermute(parts[0], "dp", forward), *parts]
+    result = jnp.concatenate(parts, axis=0)
+    shift = (lax.axis_index("dp") + 1) * parts[-1].shape[0]
+    routes = jnp.roll(result, shift, axis=0)
     capacity = MOST * lax.axis_size("dp")
     block_rows = min(128, capacity)
     window_size = w_gate.shape[0]

time: 208 us -> 236 us (1.13)
  waiting for transfers between devices: 28 us -> 73.9 us
  blocking collectives: 98.3 us -> 76 us
  starting transfers between devices: 0.01 us -> 3.17 us
    ppermute x0 -> x7, waiting for transfers between devices: none -> 37.5 us  [body(): parts = [lax.ppermute(parts[0], 'dp', forward), *parts]]
    all_gather x1 -> x0, blocking collectives: 22.7 us -> none  [body(): routes = lax.all_gather(expert_ids, 'dp', axis=0, tiled=True)]
    psum x1, waiting for transfers between devices: 28 us -> 36.4 us  [body(): lax.psum((gate_parts, up_parts, logit_part), 'seq')]
    ppermute x0 -> x7, starting transfers between devices: none -> 3.17 us  [body(): parts = [lax.ppermute(parts[0], 'dp', forward), *parts]]
  transfers between devices with their start and end apart: 1 -> 8, of which waited for: 1 -> 7; matrix products, arithmetic and copies ran while one was open for 1% -> 1% of each run, Pallas kernels for 0% -> 0%
where the time goes in v1:
time: 236 us
  blocking collectives  76 us (32%)
  waiting for transfers between devices  73.9 us (31%)
  matrix products  49.8 us (21%)
  local copies, waits for them, and re-layouts  15.6 us (7%)
  between operations  14.4 us (6%)
  starting transfers between devices  3.17 us (1%)
  other arithmetic  3.12 us (1%)
    unnamed x1, blocking collectives  39.3 us
    ppermute x7, waiting for transfers between devices, body(): parts = [lax.ppermute(parts[0], 'dp', forward), *parts]  37.5 us
    psum x1, waiting for transfers between devices, body(): lax.psum((gate_parts, up_parts, logit_part), 'seq')  36.4 us
    all_gather x1, blocking collectives, body(): gathered = lax.all_gather(tokens, 'dp', axis=0, tiled=True)  31.1 us
    dot_general x5, matrix products, body(): jnp.dot(buffers[expert], w_gate[expert], preferred_element_type=jnp.float32)  19.5 us
    dot_general x5, matrix products, body(): jnp.dot(hidden[expert], w_down[expert], preferred_element_type=jnp.float32)  18.6 us
    dot_general x5, matrix products, body(): jnp.dot(buffers[expert], w_up[expert], preferred_element_type=jnp.float32)  11.6 us
    psum x1, blocking collectives, body(): lax.psum((gate_parts, up_parts, logit_part), 'seq')  5.64 us
  transfers between devices with their start and end apart: 8, of which 7 were waited for; matrix products, arithmetic and copies ran while one was open for 1% of the time, Pallas kernels for 0%

profile of v1, /device:TPU:0, one launch (start us, length us, event | category | flops | bytes accessed | tf_op | source)
XLA Modules:
  0.0 236.0 jit_solution(12595302976390409670)
XLA Ops:
  6.5 3.0 %collective-permute-start = (s32[4,2]{0,1:T(2,128)}, s32[4,2]{0,1:T(2,128)S(1)}, u32[]{:S(2)}, u32[]{:S(2)}) collective-permute-start(s32[4,2]{0,1:T(2,128)} %param.7), channel_id=1, source_target_pairs={{0,4},{4,8},{8,12},{12,16},{16,20},{20,24},{24,28},{28,0},{1,5},{5... | collective-permute-start | bytes 104 | tf_op jit(solution)/shard_map/ppermute | solution.py:29
  9.5 31.1 %all-gather = bf16[8,4,1536]{2,1,0:T(4,128)(2,1)S(1)} all-gather(bf16[1,4,1536]{2,1,0:T(4,128)(2,1)} %bitcast.173), channel_id=1, replica_groups=mesh['dp'=8,'seq'=4] {'dp'}, dimensions={0}, use_global_device_ids=true | all-gather | bytes 110592 | tf_op jit(solution)/shard_map/all_gather | solution.py:24
  40.6 0.1 fusion.120
  40.8 5.6 %psum.21 = f32[32,8]{0,1:T(8,128)S(1)} all-reduce(f32[32,8]{0,1:T(8,128)S(1)} %fusion.120), channel_id=1, replica_groups=mesh['dp'=8,'seq'=4] {'seq'}, use_global_device_ids=true, to_apply=%region_0.1 | all-reduce | flops 256 | bytes 2048 | tf_op jit(solution)/shard_map/psum | solution.py:54
  46.4 1.2 dynamic-slice
  48.3 0.2 collective-permute-start.1
  48.5 6.1 %collective-permute-done.1 = s32[4,2]{0,1:T(2,128)S(1)} collective-permute-done((s32[4,2]{0,1:T(2,128)S(1)}, s32[4,2]{0,1:T(2,128)S(1)}, u32[]{:S(2)}, u32[]{:S(2)}) %collective-permute-start.1) | collective-permute-done | bytes 64 | tf_op jit(solution)/shard_map/ppermute | solution.py:29
  54.6 6.3 %collective-permute-done.2 = s32[4,2]{0,1:T(2,128)S(1)} collective-permute-done((s32[4,2]{0,1:T(2,128)S(1)}, s32[4,2]{0,1:T(2,128)S(1)}, u32[]{:S(2)}, u32[]{:S(2)}) %collective-permute-start.2) | collective-permute-done | bytes 64 | tf_op jit(solution)/shard_map/ppermute | solution.py:29
  60.9 6.3 %collective-permute-done.3 = s32[4,2]{0,1:T(2,128)S(1)} collective-permute-done((s32[4,2]{0,1:T(2,128)S(1)}, s32[4,2]{0,1:T(2,128)S(1)}, u32[]{:S(2)}, u32[]{:S(2)}) %collective-permute-start.3) | collective-permute-done | bytes 64 | tf_op jit(solution)/shard_map/ppermute | solution.py:29
  67.2 6.3 %collective-permute-done.4 = s32[4,2]{0,1:T(2,128)S(1)} collective-permute-done((s32[4,2]{0,1:T(2,128)S(1)}, s32[4,2]{0,1:T(2,128)S(1)}, u32[]{:S(2)}, u32[]{:S(2)}) %collective-permute-start.4) | collective-permute-done | bytes 64 | tf_op jit(solution)/shard_map/ppermute | solution.py:29
  73.5 6.3 %collective-permute-done.5 = s32[4,2]{0,1:T(2,128)S(1)} collective-permute-done((s32[4,2]{0,1:T(2,128)S(1)}, s32[4,2]{0,1:T(2,128)S(1)}, u32[]{:S(2)}, u32[]{:S(2)}) %collective-permute-start.5) | collective-permute-done | bytes 64 | tf_op jit(solution)/shard_map/ppermute | solution.py:29
  79.7 6.3 %collective-permute-done.6 = s32[4,2]{0,1:T(2,128)S(1)} collective-permute-done((s32[4,2]{0,1:T(2,128)S(1)}, s32[4,2]{0,1:T(2,128)S(1)}, u32[]{:S(2)}, u32[]{:S(2)}) %collective-permute-start.6) | collective-permute-done | bytes 64 | tf_op jit(solution)/shard_map/ppermute | solution.py:29
  86.0 0.9 concatenate.6
  87.0 0.2 compare_reduce_fusion
  87.3 0.1 copy.47
  87.4 0.1 copy.41
  87.5 0.1 copy.43
  87.6 0.1 copy.45
  87.7 0.1 copy.49
  87.9 0.1 maximum_reduce_fusion.2
  88.0 0.7 scatter_custom_fusion.2
  88.9 0.1 maximum_reduce_fusion
  89.0 0.7 scatter_custom_fusion.4
  89.9 0.1 maximum_reduce_fusion.4
  90.0 0.7 scatter_custom_fusion
  90.9 0.1 maximum_reduce_fusion.3
  91.0 0.7 scatter_custom_fusion.1
  91.9 0.1 maximum_reduce_fusion.1
  92.0 0.9 scatter_custom_fusion.3
  93.1 0.1 reshape.260
  93.2 0.7 gather_fusion.10
  93.9 0.1 reshape.263
  94.0 0.6 gather_fusion.4
  94.6 0.6 gather_fusion.3
  95.2 0.6 gather_fusion.2
  95.8 0.6 gather_fusion.1
  96.4 0.6 gather_fusion
  97.0 3.9 %fusion.48 = f32[5,16,2048]{2,1,0:T(8,128)S(1)} fusion(bf16[16,1536]{1,0:T(8,128)(2,1)S(1)} %gather_fusion, bf16[5,1536,2048]{2,1,0:T(8,128)(2,1)} %param.9), kind=kOutput, calls=%fused_computation.62 | convolution fusion | flops 100663296 | bytes 6471680 | tf_op jit(solution)/shard_map/dot_general | solution.py:47
  100.9 4.3 %fusion.78 = f32[5,16,2048]{2,1,0:T(8,128)S(1)} fusion(bf16[16,1536]{1,0:T(8,128)(2,1)S(1)} %gather_fusion, bf16[5,1536,2048]{2,1,0:T(8,128)(2,1)} %param.10), kind=kOutput, calls=%fused_computation.72 | convolution fusion | flops 100663296 | bytes 6471680 | tf_op jit(solution)/shard_map/dot_general | solution.py:48
  105.2 4.5 %fusion.54 = f32[5,16,2048]{2,1,0:T(8,128)S(1)} fusion(f32[5,16,2048]{2,1,0:T(8,128)S(1)} %fusion.48, bf16[16,1536]{1,0:T(8,128)(2,1)S(1)} %gather_fusion.1, bf16[5,1536,2048]{2,1,0:T(8,128)(2,1)} %param.9), kind=kOutput, calls=%fused_computation.64 | convolution fusion | flops 100663296 | bytes 6471680 | tf_op jit(solution)/shard_map/dot_general | solution.py:47
  109.7 4.5 %fusion.84 = f32[5,16,2048]{2,1,0:T(8,128)S(1)} fusion(f32[5,16,2048]{2,1,0:T(8,128)S(1)} %fusion.78, bf16[16,1536]{1,0:T(8,128)(2,1)S(1)} %gather_fusion.1, bf16[5,1536,2048]{2,1,0:T(8,128)(2,1)} %param.10), kind=kOutput, calls=%fused_computation.74 | convolution fusion | flops 100663296 | bytes 6471680 | tf_op jit(solution)/shard_map/dot_general | solution.py:48
  114.2 3.7 %fusion.60 = f32[5,16,2048]{2,1,0:T(8,128)S(1)} fusion(f32[5,16,2048]{2,1,0:T(8,128)S(1)} %fusion.54, bf16[16,1536]{1,0:T(8,128)(2,1)S(1)} %gather_fusion.2, bf16[5,1536,2048]{2,1,0:T(8,128)(2,1)} %param.9), kind=kOutput, calls=%fused_computation.66 | convolution fusion | flops 100663296 | bytes 6471680 | tf_op jit(solution)/shard_map/dot_general | solution.py:47
  117.9 0.9 fusion.90
  118.8 3.7 %fusion.66 = f32[5,16,2048]{2,1,0:T(8,128)S(1)} fusion(f32[5,16,2048]{2,1,0:T(8,128)S(1)} %fusion.60, bf16[16,1536]{1,0:T(8,128)(2,1)S(1)} %gather_fusion.3, bf16[5,1536,2048]{2,1,0:T(8,128)(2,1)} %param.9), kind=kOutput, calls=%fused_computation.68 | convolution fusion | flops 100663296 | bytes 6471680 | tf_op jit(solution)/shard_map/dot_general | solution.py:47
  122.6 0.9 fusion.96
  123.5 3.7 %fusion.72 = f32[5,16,2048]{2,1,0:T(8,128)S(1)} fusion(f32[5,16,2048]{2,1,0:T(8,128)S(1)} %fusion.66, bf16[16,1536]{1,0:T(8,128)(2,1)S(1)} %gather_fusion.4, bf16[5,1536,2048]{2,1,0:T(8,128)(2,1)} %param.9), kind=kOutput, calls=%fused_computation.70 | convolution fusion | flops 100663296 | bytes 6471680 | tf_op jit(solution)/shard_map/dot_general | solution.py:47
  127.2 0.9 fusion.102
  128.2 0.9 copy-done.3
  129.2 0.3 add_reduce_fusion.4
  129.4 36.4 %all-reduce.5.cloned.1.call-done = (f32[5,16,2048]{2,1,0:T(8,128)}, f32[5,16,2048]{2,1,0:T(8,128)}) async-done(((f32[5,16,2048]{2,1,0:T(8,128)}, f32[5,16,2048]{2,1,0:T(8,128)}), (f32[5,16,2048]{2,1,0:T(8,128)}, f32[5,16,2048]{2,1,0:T(8,128)})) %all-reduce.5.cloned.1.call-update) | async-done | bytes 1310736 | tf_op jit(solution)/shard_map/psum | solution.py:54
  165.9 1.5 multiply_convert_fusion
  167.3 3.7 %fusion = f32[16,1536]{1,0:T(8,128)S(1)} fusion(bf16[5,2048,1536]{2,1,0:T(8,128)(2,1)} %param.11, bf16[5,16,2048]{2,1,0:T(8,128)(2,1)S(1)} %multiply_convert_fusion), kind=kOutput, calls=%fused_computation.16 | convolution fusion | flops 100663296 | bytes 6455296 | tf_op jit(solution)/shard_map/dot_general | solution.py:61
  171.1 3.7 %fusion.2 = f32[16,1536]{1,0:T(8,128)S(1)} fusion(bf16[5,2048,1536]{2,1,0:T(8,128)(2,1)} %param.11, bf16[5,16,2048]{2,1,0:T(8,128)(2,1)S(1)} %multiply_convert_fusion), kind=kOutput, calls=%fused_computation.18 | convolution fusion | flops 100663296 | bytes 6455296 | tf_op jit(solution)/shard_map/dot_general | solution.py:61
  174.8 3.7 %fusion.4 = f32[16,1536]{1,0:T(8,128)S(1)} fusion(bf16[5,2048,1536]{2,1,0:T(8,128)(2,1)} %param.11, bf16[5,16,2048]{2,1,0:T(8,128)(2,1)S(1)} %multiply_convert_fusion), kind=kOutput, calls=%fused_computation.20 | convolution fusion | flops 100663296 | bytes 6455296 | tf_op jit(solution)/shard_map/dot_general | solution.py:61
  178.5 3.7 %fusion.6 = f32[16,1536]{1,0:T(8,128)S(1)} fusion(bf16[5,2048,1536]{2,1,0:T(8,128)(2,1)} %param.11, bf16[5,16,2048]{2,1,0:T(8,128)(2,1)S(1)} %multiply_convert_fusion), kind=kOutput, calls=%fused_computation.22 | convolution fusion | flops 100663296 | bytes 6455296 | tf_op jit(solution)/shard_map/dot_general | solution.py:61
  182.2 3.7 %fusion.8 = f32[16,1536]{1,0:T(8,128)S(1)} fusion(bf16[5,2048,1536]{2,1,0:T(8,128)(2,1)} %param.11, bf16[5,16,2048]{2,1,0:T(8,128)(2,1)S(1)} %multiply_convert_fusion), kind=kOutput, calls=%fused_computation.24 | convolution fusion | flops 100663296 | bytes 6455296 | tf_op jit(solution)/shard_map/dot_general | solution.py:61
  185.9 0.6 gather_fusion.9
  186.6 0.6 gather_fusion.8
  187.2 0.6 gather_fusion.7
  187.8 0.6 gather_fusion.5
  188.5 0.6 gather_fusion.6
  189.1 0.1 multiply_add_fusion
  189.3 39.3 %all-reduce.6 = bf16[32,1536]{1,0:T(8,128)(2,1)S(1)} all-reduce(f32[32,1536]{1,0:T(8,128)S(1)} %multiply_add_fusion), channel_id=2, replica_groups=mesh['dp'=8,'seq'=4] {'dp'}, use_global_device_ids=true, to_apply=%region_18.19.clone | all-reduce | flops 49152 | bytes 294912
  228.5 0.6 dynamic-slice_convert_fusion
  (59 shorter events, 1.3 us)
Async XLA Ops:
  6.5 34.1 %copy-start = (bf16[1536,8]{0,1:T(8,128)(2,1)S(1)}, bf16[1536,8]{0,1:T(8,128)(2,1)}, u32[]{:S(2)}) copy-start(bf16[1536,8]{0,1:T(8,128)(2,1)} %param.8) | copy-start | bytes 73732
  6.5 159.3 %all-reduce.5.cloned.1.call-start = ((), (), s32[]{:S(2)}) async-start(), calls=%async_computation | async-start | bytes 2621440 | tf_op jit(solution)/shard_map/psum | solution.py:54
  6.5 41.8 %collective-permute-start = (s32[4,2]{0,1:T(2,128)}, s32[4,2]{0,1:T(2,128)S(1)}, u32[]{:S(2)}, u32[]{:S(2)}) collective-permute-start(s32[4,2]{0,1:T(2,128)} %param.7), channel_id=1, source_target_pairs={{0,4},{4,8},{8,12},{12,16},{16,20},{20,24},{24,28},{28,0},{1,5},{5... | collective-permute-start | bytes 104 | tf_op jit(solution)/shard_map/ppermute | solution.py:29
  48.3 6.3 %collective-permute-start.1 = (s32[4,2]{0,1:T(2,128)S(1)}, s32[4,2]{0,1:T(2,128)S(1)}, u32[]{:S(2)}, u32[]{:S(2)}) collective-permute-start(s32[4,2]{0,1:T(2,128)S(1)} %collective-permute-done), channel_id=1, source_target_pairs={{0,4},{4,8},{8,12},{12,16},{16,20},{20,24},{24,28},{28,0},{1,5},{5... | collective-permute-start | bytes 104 | tf_op jit(solution)/shard_map/ppermute | solution.py:29
  54.6 6.3 %collective-permute-start.2 = (s32[4,2]{0,1:T(2,128)S(1)}, s32[4,2]{0,1:T(2,128)S(1)}, u32[]{:S(2)}, u32[]{:S(2)}) collective-permute-start(s32[4,2]{0,1:T(2,128)S(1)} %collective-permute-done.1), channel_id=1, source_target_pairs={{0,4},{4,8},{8,12},{12,16},{16,20},{20,24},{24,28},{28,0},{1,5},{5... | collective-permute-start | bytes 104 | tf_op jit(solution)/shard_map/ppermute | solution.py:29
  60.9 6.3 %collective-permute-start.3 = (s32[4,2]{0,1:T(2,128)S(1)}, s32[4,2]{0,1:T(2,128)S(1)}, u32[]{:S(2)}, u32[]{:S(2)}) collective-permute-start(s32[4,2]{0,1:T(2,128)S(1)} %collective-permute-done.2), channel_id=1, source_target_pairs={{0,4},{4,8},{8,12},{12,16},{16,20},{20,24},{24,28},{28,0},{1,5},{5... | collective-permute-start | bytes 104 | tf_op jit(solution)/shard_map/ppermute | solution.py:29
  67.2 6.3 %collective-permute-start.4 = (s32[4,2]{0,1:T(2,128)S(1)}, s32[4,2]{0,1:T(2,128)S(1)}, u32[]{:S(2)}, u32[]{:S(2)}) collective-permute-start(s32[4,2]{0,1:T(2,128)S(1)} %collective-permute-done.3), channel_id=1, source_target_pairs={{0,4},{4,8},{8,12},{12,16},{16,20},{20,24},{24,28},{28,0},{1,5},{5... | collective-permute-start | bytes 104 | tf_op jit(solution)/shard_map/ppermute | solution.py:29
  73.5 6.3 %collective-permute-start.5 = (s32[4,2]{0,1:T(2,128)S(1)}, s32[4,2]{0,1:T(2,128)S(1)}, u32[]{:S(2)}, u32[]{:S(2)}) collective-permute-start(s32[4,2]{0,1:T(2,128)S(1)} %collective-permute-done.4), channel_id=1, source_target_pairs={{0,4},{4,8},{8,12},{12,16},{16,20},{20,24},{24,28},{28,0},{1,5},{5... | collective-permute-start | bytes 104 | tf_op jit(solution)/shard_map/ppermute | solution.py:29
  79.7 6.3 %collective-permute-start.6 = (s32[4,2]{0,1:T(2,128)S(1)}, s32[4,2]{0,1:T(2,128)S(1)}, u32[]{:S(2)}, u32[]{:S(2)}) collective-permute-start(s32[4,2]{0,1:T(2,128)S(1)} %collective-permute-done.5), channel_id=1, source_target_pairs={{0,4},{4,8},{8,12},{12,16},{16,20},{20,24},{24,28},{28,0},{1,5},{5... | collective-permute-start | bytes 104 | tf_op jit(solution)/shard_map/ppermute | solution.py:29
  97.0 20.9 %copy-start.2 = (bf16[5,1536,2048]{2,1,0:T(8,128)(2,1)S(1)}, bf16[5,1536,2048]{2,1,0:T(8,128)(2,1)}, u32[]{:S(2)}) copy-start(bf16[5,1536,2048]{2,1,0:T(8,128)(2,1)} %param.10) | copy-start | bytes 94371840
  118.8 110.3 %copy-start.1 = (bf16[1536,8]{0,1:T(8,128)(2,1)S(1)}, bf16[1536,8]{0,1:T(8,128)(2,1)}, u32[]{:S(2)}) copy-start(bf16[1536,8]{0,1:T(8,128)(2,1)} %param.8) | copy-start | bytes 73732
  127.2 0.9 copy-start.4
  128.2 0.9 copy-start.3
Sparse Core Ops, SparseCore 0:
  129.2 36.6 all-reduce.4
